TPU v7x, 32 devices: a whole 2x2x4 slice. The times are simulated.
32 devices in a mesh: ctx: 8 (over y, x, core), fsdp: 4 (over z).
Axes of the slice: x: 2, y: 2, z: 4, core: 2. Of those that a mesh axis runs over, the one named last changes fastest.
Arguments:
- layer_in: bfloat16 [8, 1024, 1024], P('fsdp', 'ctx'), may hold values from -6 to 6
- cotangent: bfloat16 [8, 1024, 1024], P('fsdp', 'ctx'), may hold values from -6 to 6
- norm1_gain: bfloat16 [1024], P('fsdp'), may hold values from 0.099609375 to 1.8984375
- norm1_shift: bfloat16 [1024], P('fsdp'), may hold values from -3 to 3
- norm2_gain: bfloat16 [1024], P('fsdp'), may hold values from 0.099609375 to 1.8984375
- norm2_shift: bfloat16 [1024], P('fsdp'), may hold values from -3 to 3
- qkv_weight: bfloat16 [1024, 3072], P('fsdp'), may hold values from -4 to 4
- qv_bias: bfloat16 [2048], P('fsdp'), may hold values from -3 to 3
- key_bias: bfloat16 [256], P('fsdp'), may hold values from -3 to 3
- attn_out_weight: bfloat16 [1024, 1024], P('fsdp'), may hold values from -1.5 to 1.5
- attn_out_bias: bfloat16 [1024], P('fsdp'), may hold values from -3 to 3
- ff_in_weight: bfloat16 [1024, 4096], P('fsdp'), may hold values from -0.1875 to 0.1875
- ff_in_bias: bfloat16 [4096], P('fsdp'), may hold values from -3 to 3
- ff_out_weight: bfloat16 [1024, 4096], P('fsdp'), may hold values from -0.09375 to 0.09375
- ff_out_bias: bfloat16 [1024], P('fsdp'), may hold values from -3 to 3
Outputs:
- layer_out: bfloat16 [8, 1024, 1024], P('fsdp', 'ctx')
- input_grad: float32 [8, 1024, 1024], P('fsdp', 'ctx')
- norm1_gain_grad: float32 [1024], P('fsdp')
- norm1_shift_grad: float32 [1024], P('fsdp')
- norm2_gain_grad: float32 [1024], P('fsdp')
- norm2_shift_grad: float32 [1024], P('fsdp')
- qkv_weight_grad: float32 [1024, 3072], P('fsdp')
- qv_bias_grad: float32 [2048], P('fsdp')
- key_bias_grad: float32 [256], P('fsdp')
- attn_out_weight_grad: float32 [1024, 1024], P('fsdp')
- attn_out_bias_grad: float32 [1024], P('fsdp')
- ff_in_weight_grad: float32 [1024, 4096], P('fsdp')
- ff_in_bias_grad: float32 [4096], P('fsdp')
- ff_out_weight_grad: float32 [1024, 4096], P('fsdp')
- ff_out_bias_grad: float32 [1024], P('fsdp')
All inputs are finite; a program needn't handle non-finite values.
Results may differ from a plain program's by a relative error of at most 0.025.
Values may be sent and summed in bfloat16 or wider, within the bound.
A program may use at most 256 MiB of HBM per device.

v0:
```python
import math
import jax
import jax.numpy as jnp
from jax import lax
from jax.sharding import PartitionSpec as P

D = 1024
H = 16
HD = 64
ROT = 16
EPSILON = 1e-05


def layer_norm(inputs, gain_vec, shift_vec):
    average = jnp.mean(inputs, axis=-1, keepdims=True)
    centred = inputs - average
    variance = jnp.mean(centred * centred, axis=-1, keepdims=True)
    inverse = lax.rsqrt(variance + EPSILON)
    normed = centred * inverse
    return (normed * gain_vec + shift_vec, normed, inverse)


def norm_back(upstream, normed, inverse, gain_vec):
    gain_grad = jnp.sum(upstream * normed, axis=0)
    shift_grad = jnp.sum(upstream, axis=0)
    scaled = upstream * gain_vec
    inner = (
        scaled
        - jnp.mean(scaled, axis=-1, keepdims=True)
        - normed * jnp.mean(scaled * normed, axis=-1, keepdims=True)
    )
    return (inverse * inner, gain_grad, shift_grad)


def paired_position(row_ids, half_rows, groups):
    owner = row_ids // (2 * half_rows)
    within = row_ids % (2 * half_rows)
    late = 2 * half_rows * groups - (owner + 2) * half_rows + within
    return jnp.where(within < half_rows, owner * half_rows + within, late)


def rotary_tables(positions):
    halfway = ROT // 2
    freq_steps = jnp.arange(halfway, dtype=jnp.float32)
    frequency = jnp.exp(freq_steps * (-2.0 * math.log(10000.0) / ROT))
    theta = positions.astype(jnp.float32)[:, None] * frequency[None, :]
    return (jnp.cos(theta)[:, None, :], jnp.sin(theta)[:, None, :])


def rotate(inputs, cosine, sine):
    halfway = ROT // 2
    first = inputs[..., :halfway]
    second = inputs[..., halfway:ROT]
    return jnp.concatenate(
        [first * cosine - second * sine, second * cosine + first * sine, inputs[..., ROT:]], axis=-1
    )


def rotate_back(upstream, cosine, sine):
    halfway = ROT // 2
    first = upstream[..., :halfway]
    second = upstream[..., halfway:ROT]
    return jnp.concatenate(
        [first * cosine + second * sine, second * cosine - first * sine, upstream[..., ROT:]],
        axis=-1,
    )


def gelu_parts(inputs):
    cumulative = 0.5 * (1.0 + lax.erf(inputs * (1.0 / math.sqrt(2.0))))
    density = jnp.exp(-0.5 * inputs * inputs) * (1.0 / math.sqrt(2.0 * math.pi))
    return (inputs * cumulative, cumulative + inputs * density)


def contract_rows(left, right):
    return lax.dot_general(
        left, right, (((0,), (0,)), ((), ())), preferred_element_type=jnp.float32
    )


def contract_cols(left, right):
    return lax.dot_general(
        left, right, (((1,), (1,)), ((), ())), preferred_element_type=jnp.float32
    )


def blocked(matrix, blocks, key_block):
    seq_count = matrix.shape[0]
    return matrix.reshape(seq_count, blocks, key_block, H, HD).transpose(1, 0, 2, 3, 4)


def per_device(
    layer_in,
    cotangent,
    norm1_gain,
    norm1_shift,
    norm2_gain,
    norm2_shift,
    qkv_weight,
    qv_bias,
    key_bias,
    attn_out_weight,
    attn_out_bias,
    ff_in_weight,
    ff_in_bias,
    ff_out_weight,
    ff_out_bias,
):
    ctx_count = lax.axis_size("ctx")
    shard_count = lax.axis_size("fsdp")
    ctx_place = lax.axis_index("ctx")
    shard_place = lax.axis_index("fsdp")
    seq_count = layer_in.shape[0]
    tokens = layer_in.shape[1]
    half_rows = tokens // 2
    row_total = seq_count * tokens
    inputs_f = layer_in.reshape(row_total, D).astype(jnp.float32)
    upstream = cotangent.reshape(row_total, D)
    upstream_f = upstream.astype(jnp.float32)
    gathered = (
        lax.all_gather(norm1_gain, "fsdp", axis=0, tiled=True),
        lax.all_gather(norm1_shift, "fsdp", axis=0, tiled=True),
        lax.all_gather(norm2_gain, "fsdp", axis=0, tiled=True),
        lax.all_gather(norm2_shift, "fsdp", axis=0, tiled=True),
        lax.all_gather(qv_bias, "fsdp", axis=0, tiled=True),
        lax.all_gather(key_bias, "fsdp", axis=0, tiled=True),
        lax.all_gather(attn_out_bias, "fsdp", axis=0, tiled=True),
        lax.all_gather(ff_in_bias, "fsdp", axis=0, tiled=True),
        lax.all_gather(ff_out_bias, "fsdp", axis=0, tiled=True),
    )
    (
        gain_one,
        shift_one,
        gain_two,
        shift_two,
        query_value_bias,
        rotary_bias,
        attn_bias,
        ff_bias,
        out_bias,
    ) = [piece.astype(jnp.float32) for piece in gathered]
    key_full = jnp.concatenate(
        [rotary_bias.reshape(H, ROT), jnp.zeros((H, HD - ROT), jnp.float32)], axis=1
    ).reshape(D)
    in_bias = jnp.concatenate([query_value_bias[:D], key_full, query_value_bias[D:]])
    qkv_full, ff_in_full, attn_out_full, ff_out_full = (
        lax.all_gather(qkv_weight, "fsdp", axis=0, tiled=True),
        lax.all_gather(ff_in_weight, "fsdp", axis=0, tiled=True),
        lax.all_gather(attn_out_weight, "fsdp", axis=0, tiled=True),
        lax.all_gather(ff_out_weight, "fsdp", axis=0, tiled=True),
    )
    query_pos = paired_position(
        jnp.arange(tokens, dtype=jnp.int32) + ctx_place * tokens, half_rows, ctx_count
    )
    cosine, sine = rotary_tables(query_pos)
    normed_one, unit_one, inverse_one = layer_norm(inputs_f, gain_one, shift_one)
    normed_two, unit_two, inverse_two = layer_norm(inputs_f, gain_two, shift_two)
    one_b = normed_one.astype(jnp.bfloat16)
    two_b = normed_two.astype(jnp.bfloat16)
    projected = jnp.dot(one_b, qkv_full, preferred_element_type=jnp.float32) + in_bias
    ff_pre = jnp.dot(two_b, ff_in_full, preferred_element_type=jnp.float32) + ff_bias
    query_b = rotate(projected[:, :D].reshape(seq_count, tokens, H, HD), cosine, sine).astype(
        jnp.bfloat16
    )
    keys_b = rotate(projected[:, D : 2 * D].reshape(seq_count, tokens, H, HD), cosine, sine).astype(
        jnp.bfloat16
    )
    values_b = projected[:, 2 * D :].astype(jnp.bfloat16).reshape(seq_count, tokens, D)
    all_keys, all_values = (
        lax.all_gather(keys_b.reshape(seq_count, tokens, D), "ctx", axis=1, tiled=True),
        lax.all_gather(values_b, "ctx", axis=1, tiled=True),
    )
    key_total = all_keys.shape[1]
    key_block = math.gcd(key_total, 512)
    blocks = key_total // key_block
    key_pos = paired_position(jnp.arange(key_total, dtype=jnp.int32), half_rows, ctx_count).reshape(
        blocks, key_block
    )
    keys_blocked = blocked(all_keys, blocks, key_block)
    values_blocked = blocked(all_values, blocks, key_block)

    def block_scores(key_piece, pos_piece):
        scores = (
            jnp.einsum("sqhd,skhd->shqk", query_b, key_piece, preferred_element_type=jnp.float32)
            * 0.125
        )
        allowed = pos_piece[None, None, None, :] <= query_pos[None, None, :, None]
        return (jnp.where(allowed, scores, -1e30), allowed)

    def first_pass(state, inputs):
        highest, total = state
        scores, allowed = block_scores(inputs[0], inputs[1])
        new_high = jnp.maximum(highest, jnp.max(scores, axis=-1))
        total = total * jnp.exp(highest - new_high) + jnp.sum(
            jnp.exp(scores - new_high[..., None]), axis=-1
        )
        return ((new_high, total), None)

    start_state = (
        jnp.full((seq_count, H, tokens), -1e30, jnp.float32),
        jnp.zeros((seq_count, H, tokens), jnp.float32),
    )
    (highest, total), unused = lax.scan(first_pass, start_state, (keys_blocked, key_pos))
    log_total = highest + jnp.log(total)

    def second_pass(mixed, inputs):
        scores, allowed = block_scores(inputs[0], inputs[2])
        weights = jnp.where(allowed, jnp.exp(scores - log_total[..., None]), 0.0).astype(
            jnp.bfloat16
        )
        return (
            mixed
            + jnp.einsum("shqk,skhd->sqhd", weights, inputs[1], preferred_element_type=jnp.float32),
            None,
        )

    mixed, unused = lax.scan(
        second_pass,
        jnp.zeros((seq_count, tokens, H, HD), jnp.float32),
        (keys_blocked, values_blocked, key_pos),
    )
    attn_b = mixed.reshape(row_total, D).astype(jnp.bfloat16)
    activation, slope = gelu_parts(ff_pre)
    gelu_b = activation.astype(jnp.bfloat16)
    act_cat = jnp.concatenate([attn_b, gelu_b], axis=1)
    out_cat = jnp.concatenate([attn_out_full, ff_out_full], axis=1)
    mixture = contract_cols(act_cat, out_cat)
    layer_out = (inputs_f + mixture + attn_bias + out_bias).astype(jnp.bfloat16)
    back_cat = jnp.dot(upstream, out_cat, preferred_element_type=jnp.float32)
    dout_b = back_cat[:, :D].astype(jnp.bfloat16).reshape(seq_count, tokens, H, HD)
    dpre = back_cat[:, D:] * slope
    dpre_b = dpre.astype(jnp.bfloat16)
    delta = jnp.sum(
        dout_b.astype(jnp.float32) * attn_b.astype(jnp.float32).reshape(seq_count, tokens, H, HD),
        axis=-1,
    ).transpose(0, 2, 1)

    def query_side(dquery, inputs):
        key_piece, value_piece, pos_piece = inputs
        scores, allowed = block_scores(key_piece, pos_piece)
        probs = jnp.where(allowed, jnp.exp(scores - log_total[..., None]), 0.0)
        dprobs = jnp.einsum(
            "sqhd,skhd->shqk", dout_b, value_piece, preferred_element_type=jnp.float32
        )
        dscores = (probs * (dprobs - delta[..., None])).astype(jnp.bfloat16)
        dquery = (
            dquery
            + jnp.einsum("shqk,skhd->sqhd", dscores, key_piece, preferred_element_type=jnp.float32)
            * 0.125
        )
        return (dquery, (probs, dscores))

    zero_query = jnp.zeros((seq_count, tokens, H, HD), jnp.float32)

    def dquery_pass(dquery, inputs):
        dquery, unused_pair = query_side(dquery, inputs)
        return (dquery, None)

    dquery, unused = lax.scan(dquery_pass, zero_query, (keys_blocked, values_blocked, key_pos))
    all_query, all_dout = (
        lax.all_gather(query_b.reshape(seq_count, tokens, D), "ctx", axis=1, tiled=True),
        lax.all_gather(dout_b.reshape(seq_count, tokens, D), "ctx", axis=1, tiled=True),
    )
    all_lse, all_delta = (
        lax.all_gather(log_total, "ctx", axis=2, tiled=True),
        lax.all_gather(delta, "ctx", axis=2, tiled=True),
    )
    own_values = values_b.reshape(seq_count, tokens, H, HD)
    query_blocked = blocked(all_query, blocks, key_block)
    dout_blocked = blocked(all_dout, blocks, key_block)
    lse_blocked = all_lse.reshape(seq_count, H, blocks, key_block).transpose(2, 0, 1, 3)
    delta_blocked = all_delta.reshape(seq_count, H, blocks, key_block).transpose(2, 0, 1, 3)

    def key_pass(sums, inputs):
        key_sum, value_sum = sums
        rows_q, rows_do, rows_lse, rows_delta, pos_q = inputs
        scores = (
            jnp.einsum("sqhd,skhd->shqk", rows_q, keys_b, preferred_element_type=jnp.float32)
            * 0.125
        )
        allowed = query_pos[None, None, None, :] <= pos_q[None, None, :, None]
        probs = jnp.where(
            allowed, jnp.exp(jnp.where(allowed, scores, -1e30) - rows_lse[..., None]), 0.0
        )
        dprobs = jnp.einsum(
            "sqhd,skhd->shqk", rows_do, own_values, preferred_element_type=jnp.float32
        )
        dscores = (probs * (dprobs - rows_delta[..., None])).astype(jnp.bfloat16)
        key_sum = (
            key_sum
            + jnp.einsum("shqk,sqhd->skhd", dscores, rows_q, preferred_element_type=jnp.float32)
            * 0.125
        )
        value_sum = value_sum + jnp.einsum(
            "shqk,sqhd->skhd",
            probs.astype(jnp.bfloat16),
            rows_do,
            preferred_element_type=jnp.float32,
        )
        return ((key_sum, value_sum), None)

    (dkey_own, dvalue_own), unused = lax.scan(
        key_pass,
        (zero_query, zero_query),
        (query_blocked, dout_blocked, lse_blocked, delta_blocked, key_pos),
    )
    dquery_pre = rotate_back(dquery, cosine, sine).reshape(row_total, D)
    dkey_pre = rotate_back(dkey_own, cosine, sine)
    dvalue_rows = dvalue_own.reshape(row_total, D)
    dproj = jnp.concatenate([dquery_pre, dkey_pre.reshape(row_total, D), dvalue_rows], axis=1)
    dproj_b = dproj.astype(jnp.bfloat16)
    dnormed_one = contract_cols(dproj_b, qkv_full)
    dnormed_two = contract_cols(dpre_b, ff_in_full)
    dinput_one, gain_grad_one, shift_grad_one = norm_back(
        dnormed_one, unit_one, inverse_one, gain_one
    )
    dinput_two, gain_grad_two, shift_grad_two = norm_back(
        dnormed_two, unit_two, inverse_two, gain_two
    )
    input_grad = (upstream_f + dinput_one + dinput_two).reshape(seq_count, tokens, D)

    def make_terms(cot_left, one_left, two_left):

        def out_term(start, count):
            return contract_rows(cot_left, act_cat)

        def in_term(start, count):
            return jnp.concatenate(
                [contract_rows(one_left, dproj_b), contract_rows(two_left, dpre_b)], axis=1
            )

        return (out_term, in_term)

    row_count = D // shard_count
    out_term, in_term = make_terms(upstream, one_b, two_b)
    out_part = lax.psum_scatter(
        out_term(jnp.int32(0), row_count * lax.axis_size("fsdp")).astype(jnp.bfloat16),
        "fsdp",
        scatter_dimension=0,
        tiled=True,
    ).astype(jnp.float32)
    in_part = lax.psum_scatter(
        in_term(jnp.int32(0), row_count * lax.axis_size("fsdp")).astype(jnp.bfloat16),
        "fsdp",
        scatter_dimension=0,
        tiled=True,
    ).astype(jnp.float32)
    out_part, in_part = (
        lax.psum(out_part.astype(jnp.bfloat16), "ctx").astype(jnp.float32),
        lax.psum(in_part.astype(jnp.bfloat16), "ctx").astype(jnp.float32),
    )
    qv_grad = jnp.concatenate([jnp.sum(dquery_pre, axis=0), jnp.sum(dvalue_rows, axis=0)])
    rotary_grad = jnp.sum(dkey_pre[..., :ROT], axis=(0, 1)).reshape(H * ROT)
    cot_grad = jnp.sum(upstream_f, axis=0)
    ff_bias_grad = jnp.sum(dpre, axis=0)
    summed = lax.psum(
        (
            gain_grad_one,
            shift_grad_one,
            gain_grad_two,
            shift_grad_two,
            qv_grad,
            rotary_grad,
            cot_grad,
            ff_bias_grad,
        ),
        ("ctx", "fsdp"),
    )

    def own_share(vector):
        width = vector.shape[0] // shard_count
        return lax.dynamic_slice_in_dim(vector, shard_place * width, width, 0)

    shares = [own_share(vector) for vector in summed]
    return (
        layer_out.reshape(seq_count, tokens, D),
        input_grad,
        shares[0],
        shares[1],
        shares[2],
        shares[3],
        in_part[:, : 3 * D],
        shares[4],
        shares[5],
        out_part[:, :D],
        shares[6],
        in_part[:, 3 * D :],
        shares[7],
        out_part[:, D:],
        shares[6],
    )


def solution(mesh):
    placed = (
        P("fsdp", "ctx", None),
        P("fsdp", "ctx", None),
        P("fsdp"),
        P("fsdp"),
        P("fsdp"),
        P("fsdp"),
        P("fsdp", None),
        P("fsdp"),
        P("fsdp"),
        P("fsdp", None),
        P("fsdp"),
        P("fsdp", None),
        P("fsdp"),
        P("fsdp", None),
        P("fsdp"),
    )
    return jax.shard_map(
        per_device,
        mesh=mesh,
        in_specs=placed,
        out_specs=(
            P("fsdp", "ctx", None),
            P("fsdp", "ctx", None),
            P("fsdp"),
            P("fsdp"),
            P("fsdp"),
            P("fsdp"),
            P("fsdp", None),
            P("fsdp"),
            P("fsdp"),
            P("fsdp", None),
            P("fsdp"),
            P("fsdp", None),
            P("fsdp"),
            P("fsdp", None),
            P("fsdp"),
        ),
        check_vma=False,
    )
```

profile of v0, /device:TPU:0, one launch (start us, length us, event | category | flops | bytes accessed | tf_op | source)
XLA Modules:
  0.0 1189.8 jit_solution(6554706821487634734)
XLA Ops:
  10.1 12.7 %all-gather.1 = bf16[4,1,256]{2,1,0:T(2,128)(2,1)S(1)} all-gather(bf16[1,1,256]{2,1,0:T(2,128)(2,1)S(1)} %reshape.446), channel_id=1, replica_groups=mesh['ctx'=8,'fsdp'=4] {'fsdp'}, dimensions={0}, use_global_device_ids=true | all-gather | bytes 2560 | tf_op jit(solution)/shard_map/all_gather | solution.py:122
  22.8 8.1 all-gather
  30.9 14.0 %all-gather.4 = bf16[4,1,256]{2,1,0:T(2,128)(2,1)S(1)} all-gather(bf16[1,1,256]{2,1,0:T(2,128)(2,1)S(1)} %reshape.452), channel_id=1, replica_groups=mesh['ctx'=8,'fsdp'=4] {'fsdp'}, dimensions={0}, use_global_device_ids=true | all-gather | bytes 2560 | tf_op jit(solution)/shard_map/all_gather | solution.py:124
  45.0 8.7 all-gather.3
  55.2 10.4 all-reduce.1
  65.7 22.4 %all-gather.2 = bf16[4,1,512]{2,1,0:T(2,128)(2,1)S(1)} all-gather(bf16[1,1,512]{2,1,0:T(2,128)(2,1)S(1)} %reshape.448), channel_id=1, replica_groups=mesh['ctx'=8,'fsdp'=4] {'fsdp'}, dimensions={0}, use_global_device_ids=true | all-gather | bytes 5120 | tf_op jit(solution)/shard_map/all_gather | solution.py:125
  90.4 37.9 %all-gather.16.cloned.1.call-done = bf16[1024,3072]{1,0:T(8,128)(2,1)} async-done(((bf16[256,3072]{1,0:T(8,128)(2,1)}), bf16[1024,3072]{1,0:T(8,128)(2,1)}) %all-gather.16.cloned.1.call-update) | async-done | bytes 6291472 | tf_op jit(solution)/shard_map/all_gather | solution.py:147
  128.3 4.6 convolution_add_fusion.1
  135.8 2.9 fusion.171
  150.8 12.4 %all_gather.67 = bf16[4096]{0:T(1024)(128)(2,1)S(1)} all-gather(bf16[1024]{0:T(1024)(128)(2,1)S(1)} %copy-done.39), channel_id=1, replica_groups=mesh['ctx'=8,'fsdp'=4] {'fsdp'}, dimensions={0}, use_global_device_ids=true | all-gather | bytes 10240 | tf_op jit(solution)/shard_map/all_gather | solution.py:128
  163.2 10.6 all-gather.24.cloned.1.call-done
  173.8 3.1 constant_dynamic-update-slice_fusion.1
  177.0 146.9 %all-gather.26.cloned.1.call-done = bf16[1024,4096]{1,0:T(8,128)(2,1)} async-done(((bf16[256,4096]{1,0:T(8,128)(2,1)}), bf16[1024,4096]{1,0:T(8,128)(2,1)}) %all-gather.26.cloned.1.call-update) | async-done | bytes 8388624 | tf_op jit(solution)/shard_map/all_gather | solution.py:150
  323.8 8.3 constant_dynamic-update-slice_fusion
  332.1 6.5 convolution_bitcast_fusion
  342.8 130.3 %all-gather.22.cloned.1.call-done = bf16[1024,4096]{1,0:T(8,128)(2,1)} async-done(((bf16[256,4096]{1,0:T(8,128)(2,1)}), bf16[1024,4096]{1,0:T(8,128)(2,1)}) %all-gather.22.cloned.1.call-update) | async-done | bytes 8388624 | tf_op jit(solution)/shard_map/all_gather | solution.py:148
  473.1 9.2 fusion.167
  482.3 28.6 %all-gather.18.cloned.1.call-done = bf16[2,1024,1024]{1,2,0:T(8,128)(2,1)} async-done(((bf16[2,128,1024]{1,2,0:T(8,128)(2,1)}), bf16[2,1024,1024]{1,2,0:T(8,128)(2,1)}) %all-gather.18.cloned.1.call-update) | async-done | bytes 4194320 | tf_op jit(solution)/shard_map/all_gather | solution.py:171
  511.0 7.8 reshape.422
  518.8 5.4 copy.89
  524.2 25.9 %all-gather.20.cloned.1.call-done = bf16[2,1024,1024]{1,2,0:T(8,128)(2,1)} async-done(((bf16[2,128,1024]{1,2,0:T(8,128)(2,1)}), bf16[2,1024,1024]{1,2,0:T(8,128)(2,1)}) %all-gather.20.cloned.1.call-update) | async-done | bytes 4194320 | tf_op jit(solution)/shard_map/all_gather | solution.py:170
  550.1 7.8 reshape.424
  557.9 5.6 copy.90
  563.5 24.2 %while.48 = (s32[]{:T(128)}, f32[2,16,128]{2,1,0:T(8,128)S(1)}, f32[2,16,128]{2,1,0:T(8,128)S(1)}, s32[2,512]{1,0:T(2,128)S(1)}, bf16[2,2,512,16,64]{2,4,3,1,0:T...) while((s32[]{:T(128)}, f32[2,16,128]{2,1,0:T(8,128)S(1)}, ...), condition=%wide.region_5.6_spmd.clone, body=%wide.region_2.5_spmd.clone.sunk | while | flops 283205120 | bytes 19815548 | solution.py:203
  563.6 6.7 fusion.223
  570.3 5.2 exponential_reduce_fusion.2
  575.8 6.7 fusion.223
  582.4 5.2 exponential_reduce_fusion.2
  587.7 13.5 %while.49 = (s32[]{:T(128)}, f32[2,128,16,64]{1,3,2,0:T(8,128)}, bf16[2,2,512,16,64]{2,4,3,1,0:T(8,128)(2,1)}, s32[2,512]{1,0:T(2,128)S(1)}, bf16[2,2,512,16,64]...) while((s32[]{:T(128)}, f32[2,128,16,64]{1,3,2,0:T(8,128)}, ...), condition=%wide.region_7.8_spmd.clone, body=%wide.region_6.7_spmd.clone.sunk | while | flops 547950080 | bytes 6972030 | solution.py:217
  587.9 6.2 fusion.229
  594.2 6.4 fusion.229
  604.8 7.2 convert_bitcast_fusion
  613.9 2.8 copy.113
  617.6 7.4 convolution_convert_fusion
  625.0 30.8 %while.50 = (s32[]{:T(128)}, f32[2,128,16,64]{1,3,2,0:T(8,128)S(1)}, bf16[2,2,512,16,64]{2,4,3,1,0:T(8,128)(2,1)}, s32[2,512]{1,0:T(2,128)S(1)}, bf16[2,128,16,6...) while((s32[]{:T(128)}, ...), condition=%wide.region_10.11_spmd.clone, body=%wide.region_9.10_spmd.clone.sunk | while | flops 820841984 | bytes 26387088 | solution.py:259
  625.2 6.2 fusion.236
  631.6 8.8 fusion.237
  640.5 6.2 fusion.236
  646.9 8.9 fusion.237
  657.7 7.8 reshape.430
  665.5 5.2 copy.109
  670.7 9.3 all_gather.73
  680.1 8.4 all_gather.75
  688.6 8.0 reshape.432
  696.7 5.2 copy.112
  701.9 48.0 %while.51 = (s32[]{:T(128)}, f32[2,128,16,64]{1,3,2,0:T(8,128)S(1)}, f32[2,128,16,64]{1,3,2,0:T(8,128)}, bf16[2,2,512,16,64]{2,4,3,1,0:T(8,128)(2,1)}, s32[2,512...) while((s32[]{:T(128)}, ...), condition=%wide.region_12.13_spmd.clone, body=%wide.region_11.12_spmd.clone.sunk | while | flops 1100287488 | bytes 39723684 | solution.py:302
  701.9 6.3 fusion.245
  708.5 11.0 fusion.246
  719.5 6.3 fusion.247
  725.8 6.3 fusion.245
  732.4 10.7 fusion.246
  743.1 6.5 fusion.247
  758.9 10.5 pad_maximum_fusion
  770.0 11.4 all-gather.6
  782.0 9.6 all-gather.5
  792.9 16.3 %reduce-scatter.5.cloned.1.call-done = bf16[256,5120]{0,1:T(8,128)(2,1)} async-done(((bf16[1024,5120]{0,1:T(8,128)(2,1)}), bf16[256,5120]{0,1:T(8,128)(2,1)}) %reduce-scatter.5.cloned.1.call-update) | async-done | bytes 2621456 | tf_op jit(solution)/shard_map/reduce_scatter | solution.py:336
  809.1 248.9 %reduce-scatter.3.cloned.1.call-done = bf16[256,7168]{1,0:T(8,128)(2,1)} async-done(((bf16[1024,7168]{1,0:T(8,128)(2,1)}), bf16[256,7168]{1,0:T(8,128)(2,1)}) %reduce-scatter.3.cloned.1.call-update) | async-done | bytes 3670032 | tf_op jit(solution)/shard_map/reduce_scatter | solution.py:342
  1058.2 7.5 fusion.159
  1066.5 3.8 fusion.156
  1073.2 7.1 multiply_reduce_fusion.1
  1080.3 42.5 %all-reduce.2 = (f32[1024]{0:T(1024)S(1)}, f32[1024]{0:T(1024)S(1)}, f32[1024]{0:T(1024)S(1)}, f32[1024]{0:T(1024)S(1)}, f32[2048]{0:T(1024)S(1)}, /*index=5*/f3...) all-reduce(f32[1024]{0:T(1024)S(1)} %get-tuple-element.477, ...), channel_id=1, replica_groups=mesh['ctx'=8,'fsdp'=4] {'ctx','fsdp'}, use_global_device_ids=true, to_apply=%region_18.19 | all-reduce | flops 11520 | bytes 92160 | tf_op jit(solution)/shard_map/psum | solution.py:356
  1130.1 37.1 %all-reduce.6.cloned.1.call-done = (bf16[256,7168]{1,0:T(8,128)(2,1)}, bf16[256,5120]{0,1:T(8,128)(2,1)}) async-done(((bf16[256,7168]{1,0:T(8,128)(2,1)}, bf16[256,5120]{0,1:T(8,128)(2,1)}), (bf16[256,7168]{1,0:T(8,128)(2,1)}, bf16[256,5120]{0,1:T(8,128)(2,1)})) %all-reduce.6.cloned.1.call-update) | async-done | bytes 6291472 | tf_op jit(solution)/shard_map/psum | solution.py:350
  1167.2 3.6 slice.117
  1177.0 5.6 copy.122
  (278 shorter events, 64.0 us)
Async XLA Ops:
  7.2 46.5 %copy-start.48 = (u32[32]{0:T(128)S(1)}, u32[32]{0:T(128)}, u32[]{:S(2)}) copy-start(u32[32]{0:T(128)} %constant.185) | copy-start | bytes 388
  7.2 2.9 copy-start.41
  7.2 15.6 %copy-start.42 = (bf16[256]{0:T(256)(128)(2,1)S(1)}, bf16[256]{0:T(256)(128)(2,1)}, u32[]{:S(2)}) copy-start(bf16[256]{0:T(256)(128)(2,1)} %param.25) | copy-start | bytes 1540
  7.2 23.7 %copy-start.43 = (bf16[256]{0:T(256)(128)(2,1)S(1)}, bf16[256]{0:T(256)(128)(2,1)}, u32[]{:S(2)}) copy-start(bf16[256]{0:T(256)(128)(2,1)} %param.28) | copy-start | bytes 1540
  7.2 37.7 %copy-start.44 = (bf16[256]{0:T(256)(128)(2,1)S(1)}, bf16[256]{0:T(256)(128)(2,1)}, u32[]{:S(2)}) copy-start(bf16[256]{0:T(256)(128)(2,1)} %param.27) | copy-start | bytes 1540
  7.2 46.4 %copy-start.40 = (bf16[512]{0:T(512)(128)(2,1)S(1)}, bf16[512]{0:T(512)(128)(2,1)}, u32[]{:S(2)}) copy-start(bf16[512]{0:T(512)(128)(2,1)} %param.30) | copy-start | bytes 3076
  7.2 47.7 %copy-start.45 = (bf16[64]{0:T(256)(128)(2,1)S(1)}, bf16[64]{0:T(256)(128)(2,1)}, u32[]{:S(2)}) copy-start(bf16[64]{0:T(256)(128)(2,1)} %param.31) | copy-start | bytes 388
  7.3 80.9 %copy-start.3 = (bf16[2,128,1024]{2,1,0:T(8,128)(2,1)S(1)}, bf16[2,128,1024]{2,1,0:T(8,128)(2,1)}, u32[]{:S(2)}) copy-start(bf16[2,128,1024]{2,1,0:T(8,128)(2,1)} %param.23) | copy-start | bytes 1572868
  7.3 121.0 %all-gather.16.cloned.1.call-start = ((), (), s32[]{:S(2)}) async-start(), calls=%async_computation.2 | async-start | bytes 7864320 | tf_op jit(solution)/shard_map/all_gather | solution.py:147
  8.0 165.8 %all-gather.24.cloned.1.call-start = ((), (), s32[]{:S(2)}) async-start(), calls=%async_computation.6 | async-start | bytes 2621440 | tf_op jit(solution)/shard_map/all_gather | solution.py:149
  8.7 315.1 %all-gather.26.cloned.1.call-start = ((), (), s32[]{:S(2)}) async-start(), calls=%async_computation.7 | async-start | bytes 10485760 | tf_op jit(solution)/shard_map/all_gather | solution.py:150
  9.5 463.6 %all-gather.22.cloned.1.call-start = ((), (), s32[]{:S(2)}) async-start(), calls=%async_computation.5 | async-start | bytes 10485760 | tf_op jit(solution)/shard_map/all_gather | solution.py:148
  10.1 500.9 %all-gather.18.cloned.1.call-start = ((), (), s32[]{:S(2)}) async-start(), calls=%async_computation.3 | async-start | bytes 4718592 | tf_op jit(solution)/shard_map/all_gather | solution.py:171
  30.9 102.0 %copy-start.22 = (f32[4,1,256]{2,1,0:T(1,128)}, f32[4,1,256]{2,1,0:T(1,128)S(1)}, u32[]{:S(2)}) copy-start(f32[4,1,256]{2,1,0:T(1,128)S(1)} %convert_element_type.155) | copy-start | bytes 12292
  53.6 79.2 %copy-start.24 = (f32[4,1,256]{2,1,0:T(1,128)}, f32[4,1,256]{2,1,0:T(1,128)S(1)}, u32[]{:S(2)}) copy-start(f32[4,1,256]{2,1,0:T(1,128)S(1)} %convert_element_type.158) | copy-start | bytes 12292
  90.4 42.5 %copy-start.9 = (bf16[256,1024]{1,0:T(8,128)(2,1)}, bf16[256,1024]{1,0:T(8,128)(2,1)S(1)}, u32[]{:S(2)}) copy-start(bf16[256,1024]{1,0:T(8,128)(2,1)S(1)} %get-tuple-element.594) | copy-start | bytes 1572868
  132.9 1.7 copy-start.13
  135.6 414.5 %all-gather.20.cloned.1.call-start = ((), (), s32[]{:S(2)}) async-start(), calls=%async_computation.4 | async-start | bytes 4718592 | tf_op jit(solution)/shard_map/all_gather | solution.py:170
  135.8 9.0 copy-start.26
  135.8 9.0 copy-start.28
  144.2 6.5 copy-start.39
  148.7 509.0 %all-gather.28.cloned.1.call-start = ((), (), s32[]{:S(2)}) async-start(), calls=%async_computation.8 | async-start | bytes 4718592 | tf_op jit(solution)/shard_map/all_gather | solution.py:261
  150.7 538.0 %all-gather.30.cloned.1.call-start = ((), (), s32[]{:S(2)}) async-start(), calls=%async_computation.9 | async-start | bytes 4718592 | tf_op jit(solution)/shard_map/all_gather | solution.py:262
  177.0 155.2 %copy-start.6 = (bf16[2,128,1024]{2,1,0:T(8,128)(2,1)S(1)}, bf16[2,128,1024]{2,1,0:T(8,128)(2,1)}, u32[]{:S(2)}) copy-start(bf16[2,128,1024]{2,1,0:T(8,128)(2,1)} %param.24) | copy-start | bytes 1572868
  338.7 2.3 copy-start.5
  342.4 466.7 %reduce-scatter.5.cloned.1.call-start = ((), (), s32[]{:S(2)}) async-start(), calls=%async_computation.11 | async-start | bytes 13107200 | tf_op jit(solution)/shard_map/reduce_scatter | solution.py:336
  557.9 5.6 copy-start
  612.0 5.6 copy-start.14
  612.0 446.1 %reduce-scatter.3.cloned.1.call-start = ((), (), s32[]{:S(2)}) async-start(), calls=%async_computation.10 | async-start | bytes 18350080 | tf_op jit(solution)/shard_map/reduce_scatter | solution.py:342
  617.6 7.4 copy-start.11
  617.6 7.4 copy-start.21
  696.7 5.2 copy-start.15
  696.7 5.2 copy-start.19
  701.9 48.9 %copy-start.27 = (f32[128,8]{0,1:T(8,128)S(1)}, f32[128,8]{0,1:T(8,128)}, u32[]{:S(2)}) copy-start(f32[128,8]{0,1:T(8,128)} %copy-done.26) | copy-start | bytes 12292
  701.9 48.9 %copy-start.29 = (f32[128,8]{0,1:T(8,128)S(1)}, f32[128,8]{0,1:T(8,128)}, u32[]{:S(2)}) copy-start(f32[128,8]{0,1:T(8,128)} %copy-done.28) | copy-start | bytes 12292
  750.7 4.1 copy-start.18
  752.8 0.6 copy-start.16
  754.2 1.7 copy-start.10
  754.3 3.5 slice-start
  755.9 1.9 copy-start.12
  755.9 3.0 slice-start.1
  769.4 0.7 copy-start.46
  769.4 12.6 %copy-start.47 = (bf16[256]{0:T(256)(128)(2,1)S(1)}, bf16[256]{0:T(256)(128)(2,1)}, u32[]{:S(2)}) copy-start(bf16[256]{0:T(256)(128)(2,1)} %param.33) | copy-start | bytes 1540
  769.4 22.8 %copy-start.7 = (bf16[2,128,1024]{2,1,0:T(8,128)(2,1)S(1)}, bf16[2,128,1024]{2,1,0:T(8,128)(2,1)}, u32[]{:S(2)}) copy-start(bf16[2,128,1024]{2,1,0:T(8,128)(2,1)} %param.24) | copy-start | bytes 1572868
  769.4 397.8 %all-reduce.6.cloned.1.call-start = ((), (), s32[]{:S(2)}) async-start(), calls=%async_computation.12 | async-start | bytes 12582912 | tf_op jit(solution)/shard_map/psum | solution.py:350
  1058.1 7.6 slice-start.2
  1058.1 7.6 slice-start.3
  1058.1 7.6 slice-start.4
  1058.1 7.6 copy-start.4
  1058.2 7.6 copy-start.20
  1058.2 7.6 copy-start.36
  1058.2 7.6 copy-start.37
  1058.2 8.3 copy-start.49
  1066.5 6.6 copy-start.23
  1066.5 6.6 copy-start.25
  1073.1 7.1 copy-start.30
  1073.1 7.1 copy-start.31
  1073.1 54.1 %copy-start.8 = (bf16[2,128,1024]{2,1,0:T(8,128)(2,1)S(1)}, bf16[2,128,1024]{2,1,0:T(8,128)(2,1)}, u32[]{:S(2)}) copy-start(bf16[2,128,1024]{2,1,0:T(8,128)(2,1)} %param.24) | copy-start | bytes 1572868
  1073.1 54.1 %copy-start.17 = (f32[256,1024]{1,0:T(8,128)S(1)}, f32[256,1024]{1,0:T(8,128)}, u32[]{:S(2)}) copy-start(f32[256,1024]{1,0:T(8,128)} %fusion.159) | copy-start | bytes 3145732
  1073.2 54.1 %copy-start.33 = (f32[256]{0:T(256)S(1)}, f32[256]{0:T(256)}, u32[]{:S(2)}) copy-start(f32[256]{0:T(256)} %copy-done.32) | copy-start | bytes 3076
  1073.2 54.1 %copy-start.35 = (f32[256]{0:T(256)S(1)}, f32[256]{0:T(256)}, u32[]{:S(2)}) copy-start(f32[256]{0:T(256)} %copy-done.34) | copy-start | bytes 3076
  1125.4 57.1 %copy-start.38 = (f32[256]{0:T(256)}, f32[256]{0:T(256)S(1)}, u32[]{:S(2)}) copy-start(f32[256]{0:T(256)S(1)} %dynamic_slice.78) | copy-start | bytes 3076
  1167.2 3.6 copy-start.1
  1170.8 2.5 copy-start.2
  (2 other events, 1.2 us)
Sparse Core Ops, SparseCore 0:
  9.6 118.5 all-gather.15
  129.8 43.9 all-gather.23
  175.4 148.4 all-gather.25
  325.3 147.7 all-gather.21
  475.4 35.5 all-gather.17
  512.7 37.3 all-gather.19
  551.9 37.3 all-gather.27
  591.2 37.3 all-gather.29
  630.9 178.1 reduce-scatter.4
  811.3 246.6 reduce-scatter.2
  1061.5 105.6 all-reduce.5
where the time goes:
time: 1200 us; the launch traced here: 1190 us
  waiting for transfers between devices  685 us (57%)
  blocking collectives  170 us (14%)
  matrix products  158 us (13%)
  local copies, waits for them, and re-layouts  119 us (10%)
  other arithmetic  39.7 us (3%)
  between operations  15.8 us (1%)
    reduce_scatter x1, waiting for transfers between devices, per_device(): lax.psum_scatter(in_term(jnp.int32(0), row_count * lax.axis_size('fsdp'))...  249 us
    all_gather x1, waiting for transfers between devices, per_device(): lax.all_gather(ff_out_weight, 'fsdp', axis=0, tiled=True)  147 us
    all_gather x1, waiting for transfers between devices, per_device(): lax.all_gather(ff_in_weight, 'fsdp', axis=0, tiled=True)  130 us
    unnamed x136, local copies, waits for them, and re-layouts  45.5 us
    psum x1, blocking collectives, per_device(): lax.psum((gain_grad_one, shift_grad_one, gain_grad_two, shift_grad_two, q...  42.5 us
    all_gather x1, waiting for transfers between devices, per_device(): lax.all_gather(qkv_weight, 'fsdp', axis=0, tiled=True)  37.9 us
    psum x1, waiting for transfers between devices, per_device(): lax.psum(in_part.astype(jnp.bfloat16), 'ctx').astype(jnp.float32)  37.1 us
    reshape x4, local copies, waits for them, and re-layouts, blocked(): matrix.reshape(seq_count, blocks, key_block, H, HD).transpose(1, 0, 2, 3, 4)  31.5 us
  transfers between devices with their start and end apart: 11, of which 9 were waited for; matrix products, arithmetic and copies ran while one was open for 25% of the time, Pallas kernels for 0%

commit v1 on v0

--- a/solution.py
+++ b/solution.py
@@ -9,6 +9,25 @@
 HD = 64
 ROT = 16
 EPSILON = 1e-05
+
+
+def _drive_goods(slab_in, in_dim, peer_axis):
+    how_many = jax.lax.axis_size(peer_axis)
+    so_far_all = [slab_in]
+    for h in range(1, how_many):
+        so_far_all.append(
+            jax.lax.ppermute(
+                so_far_all[h - 1],
+                axis_name=peer_axis,
+                perm=[(at, (at - 1) % how_many) for at in range(how_many)],
+            )
+        )
+    carry_in = jnp.roll(
+        jnp.concatenate(so_far_all, in_dim),
+        shift=jax.lax.axis_index(peer_axis) * slab_in.shape[in_dim],
+        axis=in_dim,
+    )
+    return carry_in
 
 
 def layer_norm(inputs, gain_vec, shift_vec):
@@ -147,7 +166,7 @@
         lax.all_gather(qkv_weight, "fsdp", axis=0, tiled=True),
         lax.all_gather(ff_in_weight, "fsdp", axis=0, tiled=True),
         lax.all_gather(attn_out_weight, "fsdp", axis=0, tiled=True),
-        lax.all_gather(ff_out_weight, "fsdp", axis=0, tiled=True),
+        _drive_goods(ff_out_weight, 0, "fsdp"),
     )
     query_pos = paired_position(
         jnp.arange(tokens, dtype=jnp.int32) + ctx_place * tokens, half_rows, ctx_count

time: 1200 us -> 1180 us (0.983)
  waiting for transfers between devices: 685 us -> 631 us
  local copies, waits for them, and re-layouts: 119 us -> 144 us
    ppermute x0 -> x3, waiting for transfers between devices: none -> 279 us  [_drive_goods(): jax.lax.ppermute(so_far_all[h - 1], axis_name=peer_axis, perm=[(at, (at -...]
    all_gather x1 -> x0, waiting for transfers between devices: 147 us -> none  [per_device(): lax.all_gather(ff_out_weight, 'fsdp', axis=0, tiled=True)]
    all_gather x1, waiting for transfers between devices: 130 us -> 0.02 us  [per_device(): lax.all_gather(ff_in_weight, 'fsdp', axis=0, tiled=True)]
    all_gather x1, waiting for transfers between devices: 28.6 us -> 0.01 us  [per_device(): lax.all_gather(values_b, 'ctx', axis=1, tiled=True)]
    all_gather x1, waiting for transfers between devices: 25.9 us -> 8.65 us  [per_device(): lax.all_gather(keys_b.reshape(seq_count, tokens, D), 'ctx', axis=1, tiled...]
    unnamed x136 -> x132, local copies, waits for them, and re-layouts: 45.5 us -> 57.5 us
  transfers between devices with their start and end apart: 11 -> 13, of which waited for: 9 -> 8; matrix products, arithmetic and copies ran while one was open for 25% -> 28% of each run, Pallas kernels for 0% -> 0%
where the time goes in v1:
time: 1180 us; the launch traced here: 1170 us
  waiting for transfers between devices  631 us (53%)
  blocking collectives  169 us (14%)
  matrix products  161 us (14%)
  local copies, waits for them, and re-layouts  144 us (12%)
  other arithmetic  40.8 us (3%)
  between operations  15.9 us (1%)
    ppermute x3, waiting for transfers between devices, _drive_goods(): jax.lax.ppermute(so_far_all[h - 1], axis_name=peer_axis, perm=[(at, (at -...  279 us
    reduce_scatter x1, waiting for transfers between devices, per_device(): lax.psum_scatter(in_term(jnp.int32(0), row_count * lax.axis_size('fsdp'))...  249 us
    unnamed x132, local copies, waits for them, and re-layouts  57.5 us
    psum x1, blocking collectives, per_device(): lax.psum((gain_grad_one, shift_grad_one, gain_grad_two, shift_grad_two, q...  42.8 us
    all_gather x1, waiting for transfers between devices, per_device(): lax.all_gather(qkv_weight, 'fsdp', axis=0, tiled=True)  38.5 us
    psum x1, waiting for transfers between devices, per_device(): lax.psum(in_part.astype(jnp.bfloat16), 'ctx').astype(jnp.float32)  33.8 us
    reshape x4, local copies, waits for them, and re-layouts, blocked(): matrix.reshape(seq_count, blocks, key_block, H, HD).transpose(1, 0, 2, 3, 4)  31.5 us
    dot_general x4, matrix products, block_scores(): jnp.einsum('sqhd,skhd->shqk', query_b, key_piece, preferred_element_type=...  25.9 us
  transfers between devices with their start and end apart: 13, of which 8 were waited for; matrix products, arithmetic and copies ran while one was open for 28% of the time, Pallas kernels for 0%

profile of v1, /device:TPU:0, one launch (start us, length us, event | category | flops | bytes accessed | tf_op | source)
XLA Modules:
  0.0 1165.7 jit_solution(6973081452045669280)
XLA Ops:
  9.6 12.7 %all-gather.1 = bf16[4,1,256]{2,1,0:T(2,128)(2,1)S(1)} all-gather(bf16[1,1,256]{2,1,0:T(2,128)(2,1)S(1)} %reshape.446), channel_id=1, replica_groups=mesh['ctx'=8,'fsdp'=4] {'fsdp'}, dimensions={0}, use_global_device_ids=true | all-gather | bytes 2560 | tf_op jit(solution)/shard_map/all_gather | solution.py:141
  22.2 8.1 all-gather
  30.4 14.8 %all-gather.4 = bf16[4,1,256]{2,1,0:T(2,128)(2,1)S(1)} all-gather(bf16[1,1,256]{2,1,0:T(2,128)(2,1)S(1)} %reshape.452), channel_id=1, replica_groups=mesh['ctx'=8,'fsdp'=4] {'fsdp'}, dimensions={0}, use_global_device_ids=true | all-gather | bytes 2560 | tf_op jit(solution)/shard_map/all_gather | solution.py:143
  45.2 8.4 all-gather.3
  55.2 15.9 %all-reduce.1 = bf16[256]{0:T(256)(128)(2,1)S(1)} all-reduce(bf16[256]{0:T(256)(128)(2,1)S(1)} %dynamic-update-slice), channel_id=1, replica_groups=mesh['ctx'=8,'fsdp'=4] {'fsdp'}, use_global_device_ids=true, to_apply=%add.1 | all-reduce | flops 256 | bytes 1024
  71.3 16.8 %all-gather.2 = bf16[4,1,512]{2,1,0:T(2,128)(2,1)S(1)} all-gather(bf16[1,1,512]{2,1,0:T(2,128)(2,1)S(1)} %reshape.448), channel_id=1, replica_groups=mesh['ctx'=8,'fsdp'=4] {'fsdp'}, dimensions={0}, use_global_device_ids=true | all-gather | bytes 5120 | tf_op jit(solution)/shard_map/all_gather | solution.py:144
  89.8 38.5 %all-gather.15.cloned.1.call-done = bf16[1024,3072]{1,0:T(8,128)(2,1)} async-done(((bf16[256,3072]{1,0:T(8,128)(2,1)}), bf16[1024,3072]{1,0:T(8,128)(2,1)}) %all-gather.15.cloned.1.call-update) | async-done | bytes 6291472 | tf_op jit(solution)/shard_map/all_gather | solution.py:166
  128.3 4.7 convolution_add_fusion.1
  136.1 81.1 %collective-permute-done = bf16[256,4096]{1,0:T(8,128)(2,1)} collective-permute-done((bf16[256,4096]{1,0:T(8,128)(2,1)S(1)}, bf16[256,4096]{1,0:T(8,128)(2,1)}, u32[]{:S(2)}, u32[]{:S(2)}) %collective-permute-start) | collective-permute-done | bytes 2097184 | tf_op jit(solution)/shard_map/ppermute | solution.py:19
  238.6 104.2 %collective-permute-done.1 = bf16[256,4096]{1,0:T(8,128)(2,1)} collective-permute-done((bf16[256,4096]{1,0:T(8,128)(2,1)}, bf16[256,4096]{1,0:T(8,128)(2,1)}, u32[]{:S(2)}, u32[]{:S(2)}) %collective-permute-start.1) | collective-permute-done | bytes 2097184 | tf_op jit(solution)/shard_map/ppermute | solution.py:19
  347.5 3.2 constant_dynamic-update-slice_fusion.5
  350.7 93.9 %collective-permute-done.2 = bf16[256,4096]{1,0:T(8,128)(2,1)} collective-permute-done((bf16[256,4096]{1,0:T(8,128)(2,1)}, bf16[256,4096]{1,0:T(8,128)(2,1)}, u32[]{:S(2)}, u32[]{:S(2)}) %collective-permute-start.2) | collective-permute-done | bytes 2097184 | tf_op jit(solution)/shard_map/ppermute | solution.py:19
  444.5 3.2 constant_dynamic-update-slice_fusion.4
  455.5 3.3 constant_dynamic-update-slice_fusion
  458.8 7.8 constant_dynamic-slice_fusion.6
  466.6 6.3 convolution_bitcast_fusion
  476.5 12.4 %all_gather.64 = bf16[4096]{0:T(1024)(128)(2,1)S(1)} all-gather(bf16[1024]{0:T(1024)(128)(2,1)S(1)} %copy-done.37), channel_id=1, replica_groups=mesh['ctx'=8,'fsdp'=4] {'fsdp'}, dimensions={0}, use_global_device_ids=true | all-gather | bytes 10240 | tf_op jit(solution)/shard_map/all_gather | solution.py:147
  494.3 9.6 fusion.191
  503.9 7.9 reshape.422
  511.8 5.2 copy.89
  516.9 8.6 all-gather.19.cloned.1.call-done
  525.6 7.8 reshape.424
  533.4 5.5 copy.90
  538.9 24.1 %while.48 = (s32[]{:T(128)}, f32[2,16,128]{2,1,0:T(8,128)S(1)}, f32[2,16,128]{2,1,0:T(8,128)S(1)}, s32[2,512]{1,0:T(2,128)S(1)}, bf16[2,2,512,16,64]{2,4,3,1,0:T...) while((s32[]{:T(128)}, f32[2,16,128]{2,1,0:T(8,128)S(1)}, ...), condition=%wide.region_5.6_spmd.clone, body=%wide.region_2.5_spmd.clone.sunk | while | flops 283205120 | bytes 19815548 | solution.py:222
  539.1 6.6 fusion.245
  545.7 5.2 exponential_reduce_fusion.2
  551.2 6.6 fusion.245
  557.8 5.2 exponential_reduce_fusion.2
  563.1 13.2 %while.49 = (s32[]{:T(128)}, f32[2,128,16,64]{1,3,2,0:T(8,128)}, bf16[2,2,512,16,64]{2,4,3,1,0:T(8,128)(2,1)}, s32[2,512]{1,0:T(2,128)S(1)}, bf16[2,2,512,16,64]...) while((s32[]{:T(128)}, f32[2,128,16,64]{1,3,2,0:T(8,128)}, ...), condition=%wide.region_7.8_spmd.clone, body=%wide.region_6.7_spmd.clone.sunk | while | flops 547950080 | bytes 6972030 | solution.py:236
  563.3 6.2 fusion.251
  569.6 6.4 fusion.251
  581.6 7.4 convert_bitcast_fusion
  591.8 7.4 convolution_convert_fusion
  599.2 8.0 reshape.432
  607.2 5.3 copy.112
  612.5 30.9 %while.50 = (s32[]{:T(128)}, f32[2,128,16,64]{1,3,2,0:T(8,128)S(1)}, bf16[2,2,512,16,64]{2,4,3,1,0:T(8,128)(2,1)}, s32[2,512]{1,0:T(2,128)S(1)}, bf16[2,128,16,6...) while((s32[]{:T(128)}, ...), condition=%wide.region_10.11_spmd.clone, body=%wide.region_9.10_spmd.clone.sunk | while | flops 820841984 | bytes 26387088 | solution.py:278
  612.5 6.5 fusion.258
  619.1 8.9 fusion.259
  628.0 6.2 fusion.258
  634.4 8.9 fusion.259
  645.2 7.8 reshape.430
  653.0 5.3 copy.109
  658.2 9.4 all_gather.69
  667.8 8.2 all_gather.71
  676.2 48.3 %while.51 = (s32[]{:T(128)}, f32[2,128,16,64]{1,3,2,0:T(8,128)S(1)}, f32[2,128,16,64]{1,3,2,0:T(8,128)}, bf16[2,2,512,16,64]{2,4,3,1,0:T(8,128)(2,1)}, s32[2,512...) while((s32[]{:T(128)}, ...), condition=%wide.region_12.13_spmd.clone, body=%wide.region_11.12_spmd.clone.sunk | while | flops 1100287488 | bytes 39723684 | solution.py:321
  676.4 6.2 fusion.267
  682.9 11.0 fusion.268
  693.9 6.3 fusion.269
  700.2 6.3 fusion.267
  706.9 10.7 fusion.268
  717.6 6.5 fusion.269
  732.3 10.5 pad_maximum_fusion
  743.4 11.4 all-gather.6
  755.4 8.1 all-gather.5
  764.8 19.7 %reduce-scatter.5.cloned.1.call-done = bf16[256,5120]{0,1:T(8,128)(2,1)} async-done(((bf16[1024,5120]{0,1:T(8,128)(2,1)}), bf16[256,5120]{0,1:T(8,128)(2,1)}) %reduce-scatter.5.cloned.1.call-update) | async-done | bytes 2621456 | tf_op jit(solution)/shard_map/reduce_scatter | solution.py:355
  784.5 249.2 %reduce-scatter.3.cloned.1.call-done = bf16[256,7168]{1,0:T(8,128)(2,1)} async-done(((bf16[1024,7168]{1,0:T(8,128)(2,1)}), bf16[256,7168]{1,0:T(8,128)(2,1)}) %reduce-scatter.3.cloned.1.call-update) | async-done | bytes 3670032 | tf_op jit(solution)/shard_map/reduce_scatter | solution.py:361
  1033.7 7.4 fusion.182
  1045.4 6.3 fusion.176
  1051.7 42.8 %all-reduce.2 = (f32[1024]{0:T(1024)S(1)}, f32[1024]{0:T(1024)S(1)}, f32[1024]{0:T(1024)S(1)}, f32[1024]{0:T(1024)S(1)}, f32[2048]{0:T(1024)S(1)}, /*index=5*/f3...) all-reduce(f32[1024]{0:T(1024)S(1)} %get-tuple-element.477, ...), channel_id=1, replica_groups=mesh['ctx'=8,'fsdp'=4] {'ctx','fsdp'}, use_global_device_ids=true, to_apply=%region_18.19 | all-reduce | flops 11520 | bytes 92160 | tf_op jit(solution)/shard_map/psum | solution.py:375
  1098.9 3.2 fusion.172
  1102.2 6.8 fusion.180
  1108.9 33.8 %all-reduce.6.cloned.1.call-done = (bf16[256,7168]{1,0:T(8,128)(2,1)}, bf16[256,5120]{0,1:T(8,128)(2,1)}) async-done(((bf16[256,7168]{1,0:T(8,128)(2,1)}, bf16[256,5120]{0,1:T(8,128)(2,1)}), (bf16[256,7168]{1,0:T(8,128)(2,1)}, bf16[256,5120]{0,1:T(8,128)(2,1)})) %all-reduce.6.cloned.1.call-update) | async-done | bytes 6291472 | tf_op jit(solution)/shard_map/psum | solution.py:369
  1142.7 3.6 slice.117
  1152.5 5.6 copy.122
  (277 shorter events, 88.0 us)
Async XLA Ops:
  7.2 46.5 %copy-start.47 = (u32[32]{0:T(128)S(1)}, u32[32]{0:T(128)}, u32[]{:S(2)}) copy-start(u32[32]{0:T(128)} %constant.205) | copy-start | bytes 388
  7.2 2.3 copy-start.40
  7.2 15.0 %copy-start.41 = (bf16[256]{0:T(256)(128)(2,1)S(1)}, bf16[256]{0:T(256)(128)(2,1)}, u32[]{:S(2)}) copy-start(bf16[256]{0:T(256)(128)(2,1)} %param.25) | copy-start | bytes 1540
  7.2 23.1 %copy-start.42 = (bf16[256]{0:T(256)(128)(2,1)S(1)}, bf16[256]{0:T(256)(128)(2,1)}, u32[]{:S(2)}) copy-start(bf16[256]{0:T(256)(128)(2,1)} %param.28) | copy-start | bytes 1540
  7.2 38.0 %copy-start.43 = (bf16[256]{0:T(256)(128)(2,1)S(1)}, bf16[256]{0:T(256)(128)(2,1)}, u32[]{:S(2)}) copy-start(bf16[256]{0:T(256)(128)(2,1)} %param.27) | copy-start | bytes 1540
  7.2 46.4 %copy-start.38 = (bf16[512]{0:T(512)(128)(2,1)S(1)}, bf16[512]{0:T(512)(128)(2,1)}, u32[]{:S(2)}) copy-start(bf16[512]{0:T(512)(128)(2,1)} %param.30) | copy-start | bytes 3076
  7.2 47.7 %copy-start.44 = (bf16[64]{0:T(256)(128)(2,1)S(1)}, bf16[64]{0:T(256)(128)(2,1)}, u32[]{:S(2)}) copy-start(bf16[64]{0:T(256)(128)(2,1)} %param.31) | copy-start | bytes 388
  7.3 80.9 %copy-start.3 = (bf16[2,128,1024]{2,1,0:T(8,128)(2,1)S(1)}, bf16[2,128,1024]{2,1,0:T(8,128)(2,1)}, u32[]{:S(2)}) copy-start(bf16[2,128,1024]{2,1,0:T(8,128)(2,1)} %param.23) | copy-start | bytes 1572868
  7.3 121.0 %all-gather.15.cloned.1.call-start = ((), (), s32[]{:S(2)}) async-start(), calls=%async_computation.2 | async-start | bytes 7864320 | tf_op jit(solution)/shard_map/all_gather | solution.py:166
  8.0 458.6 %all-gather.23.cloned.1.call-start = ((), (), s32[]{:S(2)}) async-start(), calls=%async_computation.6 | async-start | bytes 2621440 | tf_op jit(solution)/shard_map/all_gather | solution.py:168
  8.8 485.5 %all-gather.21.cloned.1.call-start = ((), (), s32[]{:S(2)}) async-start(), calls=%async_computation.5 | async-start | bytes 10485760 | tf_op jit(solution)/shard_map/all_gather | solution.py:167
  9.5 494.4 %all-gather.17.cloned.1.call-start = ((), (), s32[]{:S(2)}) async-start(), calls=%async_computation.3 | async-start | bytes 4718592 | tf_op jit(solution)/shard_map/all_gather | solution.py:190
  30.3 97.9 %copy-start.20 = (f32[4,1,256]{2,1,0:T(1,128)}, f32[4,1,256]{2,1,0:T(1,128)S(1)}, u32[]{:S(2)}) copy-start(f32[4,1,256]{2,1,0:T(1,128)S(1)} %convert_element_type.155) | copy-start | bytes 12292
  53.7 74.6 %copy-start.22 = (f32[4,1,256]{2,1,0:T(1,128)}, f32[4,1,256]{2,1,0:T(1,128)S(1)}, u32[]{:S(2)}) copy-start(f32[4,1,256]{2,1,0:T(1,128)S(1)} %convert_element_type.158) | copy-start | bytes 12292
  88.3 40.0 %copy-start.30 = (f32[256]{0:T(256)}, f32[256]{0:T(256)S(1)}, u32[]{:S(2)}) copy-start(f32[256]{0:T(256)S(1)} %get-tuple-element.604) | copy-start | bytes 3076
  88.6 39.7 %copy-start.32 = (f32[256]{0:T(256)}, f32[256]{0:T(256)S(1)}, u32[]{:S(2)}) copy-start(f32[256]{0:T(256)S(1)} %rsqrt_bitcast_fusion) | copy-start | bytes 3076
  89.8 38.5 %copy-start.6 = (bf16[256,1024]{1,0:T(8,128)(2,1)}, bf16[256,1024]{1,0:T(8,128)(2,1)S(1)}, u32[]{:S(2)}) copy-start(bf16[256,1024]{1,0:T(8,128)(2,1)S(1)} %get-tuple-element.594) | copy-start | bytes 1572868
  128.3 7.6 copy-start.5
  133.0 1.7 copy-start.9
  135.8 389.8 %all-gather.19.cloned.1.call-start = ((), (), s32[]{:S(2)}) async-start(), calls=%async_computation.4 | async-start | bytes 4718592 | tf_op jit(solution)/shard_map/all_gather | solution.py:189
  135.8 81.3 %collective-permute-start = (bf16[256,4096]{1,0:T(8,128)(2,1)S(1)}, bf16[256,4096]{1,0:T(8,128)(2,1)}, u32[]{:S(2)}, u32[]{:S(2)}) collective-permute-start(bf16[256,4096]{1,0:T(8,128)(2,1)S(1)} %copy-done.5), channel_id=1, source_target_pairs={{0,3},{1,0},{2,1},{3,2},{4,7},{5,4},{6,5},{7,6},{8,11},{9,8},{10,9... | collective-permute-start | bytes 6291464 | tf_op jit(solution)/shard_map/ppermute | solution.py:19
  217.1 125.7 %collective-permute-start.1 = (bf16[256,4096]{1,0:T(8,128)(2,1)}, bf16[256,4096]{1,0:T(8,128)(2,1)}, u32[]{:S(2)}, u32[]{:S(2)}) collective-permute-start(bf16[256,4096]{1,0:T(8,128)(2,1)} %collective-permute-done), channel_id=1, source_target_pairs={{0,3},{1,0},{2,1},{3,2},{4,7},{5,4},{6,5},{7,6},{8,11},{9,8},{10,9... | collective-permute-start | bytes 6291464 | tf_op jit(solution)/shard_map/ppermute | solution.py:19
  219.4 15.5 %copy-start.24 = (f32[128,8]{0,1:T(8,128)}, f32[128,8]{0,1:T(8,128)S(1)}, u32[]{:S(2)}) copy-start(f32[128,8]{0,1:T(8,128)S(1)} %get-tuple-element.602) | copy-start | bytes 12292
  219.4 15.5 %copy-start.26 = (f32[128,8]{0,1:T(8,128)}, f32[128,8]{0,1:T(8,128)S(1)}, u32[]{:S(2)}) copy-start(f32[128,8]{0,1:T(8,128)S(1)} %get-tuple-element.603) | copy-start | bytes 12292
  238.6 360.6 %all-gather.27.cloned.1.call-start = ((), (), s32[]{:S(2)}) async-start(), calls=%async_computation.8 | async-start | bytes 4718592 | tf_op jit(solution)/shard_map/all_gather | solution.py:281
  342.8 101.7 %collective-permute-start.2 = (bf16[256,4096]{1,0:T(8,128)(2,1)}, bf16[256,4096]{1,0:T(8,128)(2,1)}, u32[]{:S(2)}, u32[]{:S(2)}) collective-permute-start(bf16[256,4096]{1,0:T(8,128)(2,1)} %collective-permute-done.1), channel_id=1, source_target_pairs={{0,3},{1,0},{2,1},{3,2},{4,7},{5,4},{6,5},{7,6},{8,11},{9,8},{10,9... | collective-permute-start | bytes 6291464 | tf_op jit(solution)/shard_map/ppermute | solution.py:19
  458.8 7.8 copy-start.10
  466.6 9.9 copy-start.37
  472.9 2.4 copy-start.19
  475.3 17.2 %copy-start.17 = (bf16[2,128,16,8]{1,0,3,2:T(2,128)(2,1)S(1)}, bf16[2,128,16,8]{1,0,3,2:T(2,128)(2,1)}, u32[]{:S(2)}) copy-start(bf16[2,128,16,8]{1,0,3,2:T(2,128)(2,1)} %get-tuple-element.588) | copy-start | bytes 196612
  475.3 17.2 %copy-start.18 = (bf16[2,128,16,8]{1,0,3,2:T(2,128)(2,1)S(1)}, bf16[2,128,16,8]{1,0,3,2:T(2,128)(2,1)}, u32[]{:S(2)}) copy-start(bf16[2,128,16,8]{1,0,3,2:T(2,128)(2,1)} %get-tuple-element.589) | copy-start | bytes 196612
  476.4 168.7 %all-gather.25.cloned.1.call-start = ((), (), s32[]{:S(2)}) async-start(), calls=%async_computation.7 | async-start | bytes 4718592 | tf_op jit(solution)/shard_map/all_gather | solution.py:280
  494.2 290.3 %reduce-scatter.5.cloned.1.call-start = ((), (), s32[]{:S(2)}) async-start(), calls=%async_computation.10 | async-start | bytes 13107200 | tf_op jit(solution)/shard_map/reduce_scatter | solution.py:355
  533.4 5.5 copy-start
  589.1 444.6 %reduce-scatter.3.cloned.1.call-start = ((), (), s32[]{:S(2)}) async-start(), calls=%async_computation.9 | async-start | bytes 18350080 | tf_op jit(solution)/shard_map/reduce_scatter | solution.py:361
  607.2 5.3 copy-start.8
  607.2 5.3 copy-start.16
  653.0 23.2 %copy-start.12 = (f32[2,128,16,64]{1,3,2,0:T(8,128)S(1)}, f32[2,128,16,64]{1,3,2,0:T(8,128)}, u32[]{:S(2)}) copy-start(f32[2,128,16,64]{1,3,2,0:T(8,128)} %custom-call.4) | copy-start | bytes 3145732
  676.2 49.3 %copy-start.25 = (f32[128,8]{0,1:T(8,128)S(1)}, f32[128,8]{0,1:T(8,128)}, u32[]{:S(2)}) copy-start(f32[128,8]{0,1:T(8,128)} %copy-done.24) | copy-start | bytes 12292
  676.2 49.3 %copy-start.27 = (f32[128,8]{0,1:T(8,128)S(1)}, f32[128,8]{0,1:T(8,128)}, u32[]{:S(2)}) copy-start(f32[128,8]{0,1:T(8,128)} %copy-done.26) | copy-start | bytes 12292
  725.3 3.5 copy-start.14
  727.5 2.2 copy-start.13
  728.2 1.8 copy-start.7
  728.3 3.5 slice-start
  729.9 2.3 slice-start.1
  742.8 0.7 copy-start.45
  742.8 12.6 %copy-start.46 = (bf16[256]{0:T(256)(128)(2,1)S(1)}, bf16[256]{0:T(256)(128)(2,1)}, u32[]{:S(2)}) copy-start(bf16[256]{0:T(256)(128)(2,1)} %param.33) | copy-start | bytes 1540
  742.8 21.4 %copy-start.11 = (bf16[2,128,1024]{2,1,0:T(8,128)(2,1)S(1)}, bf16[2,128,1024]{2,1,0:T(8,128)(2,1)}, u32[]{:S(2)}) copy-start(bf16[2,128,1024]{2,1,0:T(8,128)(2,1)} %param.24) | copy-start | bytes 1572868
  742.8 399.9 %all-reduce.6.cloned.1.call-start = ((), (), s32[]{:S(2)}) async-start(), calls=%async_computation.11 | async-start | bytes 12582912 | tf_op jit(solution)/shard_map/psum | solution.py:369
  1033.7 11.7 %copy-start.4 = (bf16[2,128,1024]{2,1,0:T(8,128)(2,1)S(1)}, bf16[2,128,1024]{2,1,0:T(8,128)(2,1)}, u32[]{:S(2)}) copy-start(bf16[2,128,1024]{2,1,0:T(8,128)(2,1)} %param.23) | copy-start | bytes 1572868
  1033.7 11.7 %copy-start.21 = (f32[4,1,256]{2,1,0:T(1,128)S(1)}, f32[4,1,256]{2,1,0:T(1,128)}, u32[]{:S(2)}) copy-start(f32[4,1,256]{2,1,0:T(1,128)} %copy-done.20) | copy-start | bytes 12292
  1033.7 11.6 copy-start.23
  1045.3 6.3 copy-start.28
  1045.4 6.3 copy-start.29
  1045.4 53.6 %copy-start.31 = (f32[256]{0:T(256)S(1)}, f32[256]{0:T(256)}, u32[]{:S(2)}) copy-start(f32[256]{0:T(256)} %copy-done.30) | copy-start | bytes 3076
  1045.4 53.6 %copy-start.33 = (f32[256]{0:T(256)S(1)}, f32[256]{0:T(256)}, u32[]{:S(2)}) copy-start(f32[256]{0:T(256)} %copy-done.32) | copy-start | bytes 3076
  1051.7 50.5 %copy-start.15 = (bf16[256,1024]{1,0:T(8,128)(2,1)S(1)}, bf16[256,1024]{1,0:T(8,128)(2,1)}, u32[]{:S(2)}) copy-start(bf16[256,1024]{1,0:T(8,128)(2,1)} %copy.93) | copy-start | bytes 1572868
  1051.7 50.5 %copy-start.34 = (f32[4,1,256]{2,1,0:T(1,128)S(1)}, f32[4,1,256]{2,1,0:T(1,128)}, u32[]{:S(2)}) copy-start(f32[4,1,256]{2,1,0:T(1,128)} %convert_element_type.161) | copy-start | bytes 12292
  1051.7 50.5 %copy-start.35 = (f32[4,1,256]{2,1,0:T(1,128)S(1)}, f32[4,1,256]{2,1,0:T(1,128)}, u32[]{:S(2)}) copy-start(f32[4,1,256]{2,1,0:T(1,128)} %convert_element_type.160) | copy-start | bytes 12292
  1094.5 7.7 copy-start.39
  1097.1 61.0 %copy-start.36 = (f32[256]{0:T(256)}, f32[256]{0:T(256)S(1)}, u32[]{:S(2)}) copy-start(f32[256]{0:T(256)S(1)} %dynamic_slice.83) | copy-start | bytes 3076
  1142.7 3.6 copy-start.1
  1146.3 2.5 copy-start.2
Sparse Core Ops, SparseCore 0:
  9.6 118.5 all-gather.14
  129.8 73.7 all-gather.22
  205.2 239.3 all-gather.20
  446.9 39.4 all-gather.16
  488.1 37.4 all-gather.18
  527.3 37.3 all-gather.26
  566.6 37.3 all-gather.24
  606.3 178.1 reduce-scatter.4
  786.8 246.7 reduce-scatter.2
  1036.9 105.8 all-reduce.5
